TPU v7x, 128 devices: a whole 4x4x4 slice. The times are simulated.
128 devices in a mesh: bx: 16 (over x, z), by: 8 (over y, core).
Axes of the slice: x: 4, y: 4, z: 4, core: 2. Of those that a mesh axis runs over, the one named last changes fastest.
Arguments:
- features: bfloat16 [16, 8, 1024, 128], P('bx', 'by'), may hold values from -13 to 13
- live_count: int32 [16, 8], P('bx', 'by'), may hold values from 128 to 1024, as said below
- neighbour_map: int32 [16, 8, 27, 1024], P('bx', 'by'), may hold values from 0 to 2175, as said below
- send_rows: int32 [16, 8, 8, 128], P('bx', 'by'), may hold values from 0 to 1023, as said below
- weight: bfloat16 [3456, 128], replicated, may hold values from -0.109375 to 0.109375
- gain: float32 [128], replicated, may hold values from 0.5 to 1.5
- shift: float32 [128], replicated, may hold values from -3 to 3
- cotangent: bfloat16 [16, 8, 1024, 128], P('bx', 'by'), may hold values from -13 to 13
Outputs:
- activated: bfloat16 [16, 8, 1024, 128], P('bx', 'by')
- grad_features: bfloat16 [16, 8, 1024, 128], P('bx', 'by')
- grad_weight: float32 [27, 128, 128], P(None, 'bx', 'by')
Inputs may be any that keep to these rules, and one draw needn't show every extreme that they name: Rows 0 to live_count - 1 of a brick are live, the rest padding; in every draw some brick is full. `send_rows`: every entry is below its brick's live count; the eight blocks follow the directions (dx, dy) in row-major order with the brick's own position left out. `neighbour_map`: entries index the brick's extended table; offset 13 of a live row names that row itself; every entry of a padding row is 1536. With B = min(1024, 512) and q = r // B for a live row r, an entry below 1024 lies in rows q B to q B + B - 1, and an entry 1024 + b * 128 + h of incoming block b other than 4 has h in q * 128 B / 1024 to (q + 1) * 128 B / 1024 - 1.
All inputs are finite; a program needn't handle non-finite values.
Results may differ from a plain program's by a relative error of at most 0.029.
The roundings to bfloat16 on the way count: a program that leaves them out, or rounds other values in their place, can miss the bound.
Values may be sent and summed in bfloat16 or wider, within the bound.
No kernel may reach another device: no remote copies, remote signals or barrier semaphores. Data moves between devices by JAX's collectives and lax.ppermute only.
A program may use at most 64 MiB of HBM per device.

v0:
```python
import jax
import jax.numpy as jnp
from jax import lax
from jax.sharding import PartitionSpec as P

epsilon = 1e-05


def extended(cells, sides, width):
    for axis, dim in sides:
        count = lax.axis_size(axis)
        ends = count - 1
        head = lax.slice_in_dim(cells, 0, width, axis=dim)
        tail = lax.slice_in_dim(cells, cells.shape[dim] - width, cells.shape[dim], axis=dim)
        cells = jnp.concatenate(
            [
                lax.ppermute(tail, axis, [(i, (i + 1) % count) for i in range(ends)]),
                cells,
                lax.ppermute(head, axis, [((i + 1) % count, i) for i in range(ends)]),
            ],
            axis=dim,
        )
    return cells


def from_neighbours(outgoing):
    padded = extended(outgoing, (("bx", 0), ("by", 1)), 1)
    return padded[::2, ::2]


def per_device(features, live_count, neighbour_map, send_rows, weight, gain, shift, cotangent):
    own_rows = features[0, 0]
    rows_total, channels = own_rows.shape
    halo_rows = send_rows.shape[3]
    block_rows = min(rows_total, 512)
    blocks_count = rows_total // block_rows
    halo_window = halo_rows // blocks_count
    window_rows = block_rows + 9 * halo_window
    sent_index = send_rows[0, 0].reshape(-1)
    send_select = (
        sent_index[:, None] == lax.broadcasted_iota(jnp.int32, (1, rows_total), 1)
    ).astype(jnp.bfloat16)
    chosen_rows = jnp.dot(send_select, own_rows, preferred_element_type=jnp.float32).astype(
        jnp.bfloat16
    )
    chosen_rows = chosen_rows.reshape(8, halo_rows, channels)
    blank_block = jnp.zeros((1, halo_rows, channels), jnp.bfloat16)
    outgoing = jnp.concatenate([chosen_rows[:4], blank_block, chosen_rows[4:]], axis=0).reshape(
        3, 3, halo_rows, channels
    )
    incoming = from_neighbours(outgoing).reshape(9, blocks_count, halo_window, channels)
    index_blocks = neighbour_map[0, 0].reshape(27, blocks_count, block_rows).transpose(1, 0, 2)
    own_blocks = own_rows.reshape(blocks_count, block_rows, channels)
    halo_blocks = incoming.transpose(1, 0, 2, 3)
    block_ids = jnp.arange(blocks_count, dtype=jnp.int32)

    def selector_of(indices, block_index):
        beyond = indices - rows_total
        target = beyond // halo_rows
        inside = beyond - target * halo_rows - block_index * halo_window
        local_pos = indices - block_index * block_rows
        remote_pos = block_rows + target * halo_window + inside
        usable = (inside >= 0) & (inside < halo_window)
        position = jnp.where(indices < rows_total, local_pos, jnp.where(usable, remote_pos, -1))
        return position[:, :, None] == lax.broadcasted_iota(jnp.int32, (1, 1, window_rows), 2)

    def forward_block(pieces):
        indices, own_part, halo_part, block_index = pieces
        window = jnp.concatenate([own_part, halo_part.reshape(9 * halo_window, channels)], axis=0)
        selector = selector_of(indices, block_index).astype(jnp.bfloat16)
        gathered = jnp.einsum(
            "kbw,wc->bkc", selector, window, preferred_element_type=jnp.float32
        ).astype(jnp.bfloat16)
        columns = gathered.reshape(block_rows, 27 * channels)
        return (jnp.dot(columns, weight, preferred_element_type=jnp.float32), columns)

    conv_blocks, column_blocks = lax.map(
        forward_block, (index_blocks, own_blocks, halo_blocks, block_ids)
    )
    conv_out = conv_blocks.reshape(rows_total, channels).astype(jnp.bfloat16)
    conv_float = conv_out.astype(jnp.float32)
    live_mask = (lax.broadcasted_iota(jnp.int32, (rows_total, 1), 0) < live_count[0, 0]).astype(
        jnp.float32
    )
    local_count = jnp.sum(live_mask)
    total_sum, total_count = lax.psum(
        (jnp.sum(conv_float * live_mask, axis=0), local_count), ("bx", "by")
    )
    center = total_sum / total_count
    deviation = (conv_float - center) * live_mask
    variance = lax.psum(jnp.sum(deviation * deviation, axis=0), ("bx", "by")) / total_count
    inverse_std = lax.rsqrt(variance + epsilon)
    normalized = (conv_float - center) * inverse_std
    before = gain * normalized + shift
    activated = (jnp.maximum(before, 0.0) * live_mask).astype(jnp.bfloat16)
    upstream = cotangent[0, 0].astype(jnp.float32) * (before > 0.0) * live_mask
    sum_up, sum_cross = lax.psum(
        (jnp.sum(upstream, axis=0), jnp.sum(upstream * normalized, axis=0)), ("bx", "by")
    )
    conv_grad = (
        gain
        * inverse_std
        * (upstream - live_mask * (sum_up + normalized * sum_cross) / total_count)
    ).astype(jnp.bfloat16)
    grad_blocks = conv_grad.reshape(blocks_count, block_rows, channels)

    def backward_block(weight_acc, pieces):
        indices, columns, grad_rows, block_index = pieces
        weight_acc = weight_acc + lax.dot_general(
            columns, grad_rows, (((0,), (0,)), ((), ())), preferred_element_type=jnp.float32
        )
        column_grad = lax.dot_general(
            grad_rows, weight, (((1,), (1,)), ((), ())), preferred_element_type=jnp.float32
        )
        column_grad = column_grad.reshape(block_rows, 27, channels)
        selector = selector_of(indices, block_index).astype(jnp.float32)
        window_grad = jnp.einsum(
            "kbw,bkc->wc",
            selector,
            column_grad,
            precision=lax.Precision.HIGHEST,
            preferred_element_type=jnp.float32,
        )
        return (
            weight_acc,
            (window_grad[:block_rows], window_grad[block_rows:].reshape(9, halo_window, channels)),
        )

    start_acc = jnp.zeros((27 * channels, channels), jnp.float32)
    weight_acc, (own_parts, halo_parts) = lax.scan(
        backward_block, start_acc, (index_blocks, column_blocks, grad_blocks, block_ids)
    )
    weight_terms = weight_acc.reshape(27, channels, channels)
    partial_x = lax.psum_scatter(
        weight_terms.astype(jnp.bfloat16), "bx", scatter_dimension=1, tiled=True
    )
    summed = lax.psum_scatter(partial_x, "by", scatter_dimension=2, tiled=True).astype(jnp.float32)
    grad_weight = summed / jnp.sqrt(total_count)
    own_table = own_parts.reshape(rows_total, channels)
    halo_table = halo_parts.transpose(1, 0, 2, 3).reshape(3, 3, halo_rows, channels)
    halo_grad = halo_table.astype(jnp.bfloat16)
    returned = from_neighbours(halo_grad).reshape(9, halo_rows, channels)
    slots_back = (
        jnp.concatenate([returned[:4], returned[5:]], axis=0)
        .reshape(-1, channels)
        .astype(jnp.float32)
    )
    added_back = lax.dot_general(
        send_select.astype(jnp.float32),
        slots_back,
        (((0,), (0,)), ((), ())),
        precision=lax.Precision.HIGHEST,
        preferred_element_type=jnp.float32,
    )
    own_grad = own_table + added_back
    return (activated[None, None], own_grad.astype(jnp.bfloat16)[None, None], grad_weight)


def solution(mesh):
    return jax.shard_map(
        per_device,
        mesh=mesh,
        in_specs=(
            P("bx", "by", None, None),
            P("bx", "by"),
            P("bx", "by", None, None),
            P("bx", "by", None, None),
            P(),
            P(),
            P(),
            P("bx", "by", None, None),
        ),
        out_specs=(P("bx", "by", None, None), P("bx", "by", None, None), P(None, "bx", "by")),
        check_vma=False,
    )
```

profile of v0, /device:TPU:0, one launch (start us, length us, event | category | flops | bytes accessed | tf_op | source)
XLA Modules:
  0.0 465.1 jit_solution(409183118276341036)
XLA Ops:
  7.2 1.9 fusion.34
  9.1 3.9 collective-permute-start
  13.0 1.3 collective-permute-start.1
  15.2 4.3 collective-permute-done.1
  19.5 0.8 pad_maximum_fusion.9
  20.3 1.9 collective-permute-start.2
  22.2 1.3 collective-permute-start.3
  23.6 1.2 reduce.4
  25.5 1.5 collective-permute-done.3
  27.0 1.1 pad_maximum_fusion
  28.2 38.2 %while.33 = (s32[]{:T(128)}, bf16[2,512,128]{2,1,0:T(8,128)(2,1)S(1)}, bf16[2,512,3456]{1,2,0:T(8,128)(2,1)}, bf16[2,512,128]{2,1,0:T(8,128)(2,1)}, bf16[2,9,64,...) while((s32[]{:T(128)}, ...), condition=%wide.region_1.2_spmd.clone, body=%wide.region_0.1_spmd.sunk.clone | while | flops 4321123840 | bytes 16304801 | solution.py:77
  30.2 0.9 dynamic-slice_bitcast_fusion.3
  31.2 13.0 %fusion.82 = bf16[128,27,512]{2,0,1:T(8,128)(2,1)S(1)} fusion(s32[27,512]{1,0:T(8,128)S(1)} %bitcast_select_fusion.6, bf16[576,128]{1,0:T(8,128)(2,1)S(1)} %bitcast.223, bf16[512,128]{1,0:T(8,128)(2,1)S(1)} %dynamic-slice_bitcast_fusion.3), kind=kOutput, calls=%fused_computation.3.clone.1.clone | convolution fusion | flops 3867738112 | bytes 3872768 | tf_op jit(solution)/shard_map/while/body/eval_jaxpr/kbw,wc->bkc/dot_general | solution.py:71
  44.1 2.0 constant_dynamic-update-slice_fusion.6
  46.1 1.2 fusion.83
  49.3 0.9 dynamic-slice_bitcast_fusion.3
  50.2 13.0 %fusion.82 = bf16[128,27,512]{2,0,1:T(8,128)(2,1)S(1)} fusion(s32[27,512]{1,0:T(8,128)S(1)} %bitcast_select_fusion.6, bf16[576,128]{1,0:T(8,128)(2,1)S(1)} %bitcast.223, bf16[512,128]{1,0:T(8,128)(2,1)S(1)} %dynamic-slice_bitcast_fusion.3), kind=kOutput, calls=%fused_computation.3.clone.1.clone | convolution fusion | flops 3867738112 | bytes 3872768 | tf_op jit(solution)/shard_map/while/body/eval_jaxpr/kbw,wc->bkc/dot_general | solution.py:71
  63.2 2.0 constant_dynamic-update-slice_fusion.6
  65.2 1.2 fusion.83
  66.6 70.3 %all-reduce.2 = (f32[128]{0:T(128)S(1)}, f32[]{:T(128)}) all-reduce(f32[128]{0:T(128)S(1)} %multiply_reduce_fusion.1, f32[]{:T(128)} %fusion.44), channel_id=1, replica_groups=mesh['bx'=16,'by'=8] {'bx','by'}, use_global_device_ids=true, to_apply=%region_3.4 | all-reduce | flops 129 | bytes 1032 | tf_op jit(solution)/shard_map/psum | solution.py:86
  137.8 62.7 %psum.37 = f32[128]{0:T(128)S(1)} all-reduce(f32[128]{0:T(128)S(1)} %multiply_reduce_fusion), channel_id=1, replica_groups=mesh['bx'=16,'by'=8] {'bx','by'}, use_global_device_ids=true, to_apply=%region_7.8 | all-reduce | flops 128 | bytes 1024 | tf_op jit(solution)/shard_map/psum | solution.py:91
  201.2 1.2 fusion.39
  202.4 64.2 %all-reduce.1 = (f32[128]{0:T(128)S(1)}, f32[128]{0:T(128)S(1)}) all-reduce(f32[128]{0:T(128)S(1)} %get-tuple-element.329, f32[128]{0:T(128)S(1)} %get-tuple-element.328), channel_id=1, replica_groups=mesh['bx'=16,'by'=8] {'bx','by'}, use_global_device_ids=true, to_apply=%region_11.12 | all-reduce | flops 256 | bytes 2048 | tf_op jit(solution)/shard_map/psum | solution.py:97
  266.6 1.9 fusion.42
  268.5 73.1 %while.34 = (s32[]{:T(128)}, f32[3456,128]{1,0:T(8,128)S(1)}, f32[2,512,128]{2,1,0:T(8,128)}, bf16[2,9,64,128]{3,2,0,1:T(8,128)(2,1)}, bf16[2,512,3456]{1,2,0:T(...) while((s32[]{:T(128)}, f32[3456,128]{1,0:T(8,128)S(1)}, ...), condition=%wide.region_13.14_spmd.clone.clone, body=%wide.region_12.13_spmd.clone.sunk.clone | while | flops 24024522752 | bytes 28413672 | solution.py:130
  270.5 1.1 fusion.89
  271.6 28.7 %fusion.90 = f32[1088,128]{1,0:T(8,128)S(1)} fusion(f32[512,27,128]{2,0,1:T(8,128)S(1)} %fusion.89, s32[27,512]{1,0:T(8,128)S(1)} %bitcast_select_fusion.7), kind=kOutput, calls=%fused_computation.31.clone.1.clone | convolution fusion | flops 23117266944 | bytes 7690240 | tf_op jit(solution)/shard_map/while/body/eval_jaxpr/kbw,bkc->wc/dot_general | solution.py:117
  301.8 3.2 convolution_add_fusion.3
  307.1 1.1 fusion.89
  308.2 28.7 %fusion.90 = f32[1088,128]{1,0:T(8,128)S(1)} fusion(f32[512,27,128]{2,0,1:T(8,128)S(1)} %fusion.89, s32[27,512]{1,0:T(8,128)S(1)} %bitcast_select_fusion.7), kind=kOutput, calls=%fused_computation.31.clone.1.clone | convolution fusion | flops 23117266944 | bytes 7690240 | tf_op jit(solution)/shard_map/while/body/eval_jaxpr/kbw,bkc->wc/dot_general | solution.py:117
  338.4 3.2 convolution_add_fusion.3
  341.7 1.0 convert_element_type.131
  342.8 1.0 fusion.48
  343.7 1.3 collective-permute-start.4
  345.0 1.3 collective-permute-start.5
  348.3 4.0 collective-permute-done.5
  352.3 1.0 pad_maximum_fusion.6
  353.3 1.5 collective-permute-start.6
  354.8 1.3 collective-permute-start.7
  356.1 0.9 multiply_convert_fusion
  357.1 2.2 collective-permute-done.7
  359.3 1.1 pad_maximum_fusion.1
  360.5 64.4 %all-reduce.5.cloned.1.call-done = bf16[27,128,128]{2,1,0:T(8,128)(2,1)} async-done(((bf16[27,128,128]{2,1,0:T(8,128)(2,1)}), bf16[27,128,128]{2,1,0:T(8,128)(2,1)}) %all-reduce.5.cloned.1.call-update) | async-done | bytes 884752
  424.9 0.8 constant_dynamic-slice_fusion.1
  425.7 0.9 copy.30
  426.7 3.2 fusion.35
  429.9 27.0 %reduce-scatter.3.cloned.1.call-done = bf16[27,8,16]{0,1,2:T(8,128)(2,1)} async-done(((bf16[27,8,128]{0,1,2:T(8,128)(2,1)}), bf16[27,8,16]{0,1,2:T(8,128)(2,1)}) %reduce-scatter.3.cloned.1.call-update) | async-done | bytes 6928 | tf_op jit(solution)/shard_map/reduce_scatter | solution.py:137
  456.9 0.8 convert_divide_fusion
  (68 shorter events, 9.9 us)
Async XLA Ops:
  7.2 21.0 %copy-start = (bf16[3456,128]{1,0:T(8,128)(2,1)S(1)}, bf16[3456,128]{1,0:T(8,128)(2,1)}, u32[]{:S(2)}) copy-start(bf16[3456,128]{1,0:T(8,128)(2,1)} %param.16) | copy-start | bytes 2654212
  7.2 417.8 %all-reduce.5.cloned.1.call-start = ((), (), s32[]{:S(2)}) async-start(), calls=%async_computation.2 | async-start | bytes 1769472
  9.1 6.1 %collective-permute-start = (bf16[1,3,128,128]{3,2,1,0:T(8,128)(2,1)S(1)}, bf16[1,3,128,128]{3,2,1,0:T(8,128)(2,1)S(1)}, u32[]{:S(2)}, u32[]{:S(2)}) collective-permute-start(bf16[1,3,128,128]{3,2,1,0:T(8,128)(2,1)S(1)} %bitcast.239), channel_id=1, source_target_pairs={{0,8},{8,16},{16,24},{24,32},{32,40},{40,48},{48,56},{56,64},{64,7... | collective-permute-start | bytes 294920 | tf_op jit(solution)/shard_map/ppermute | solution.py:17
  13.0 6.5 %collective-permute-start.1 = (bf16[1,3,128,128]{3,2,1,0:T(8,128)(2,1)S(1)}, bf16[1,3,128,128]{3,2,1,0:T(8,128)(2,1)S(1)}, u32[]{:S(2)}, u32[]{:S(2)}) collective-permute-start(bf16[1,3,128,128]{3,2,1,0:T(8,128)(2,1)S(1)} %bitcast.238), channel_id=1, source_target_pairs={{8,0},{16,8},{24,16},{32,24},{40,32},{48,40},{56,48},{64,56},{72,6... | collective-permute-start | bytes 294920 | tf_op jit(solution)/shard_map/ppermute | solution.py:19
  20.3 5.2 %collective-permute-start.2 = (bf16[5,1,128,128]{3,2,1,0:T(8,128)(2,1)}, bf16[5,1,128,128]{3,2,1,0:T(8,128)(2,1)}, u32[]{:S(2)}, u32[]{:S(2)}) collective-permute-start(bf16[5,1,128,128]{3,2,1,0:T(8,128)(2,1)} %get-tuple-element.372), channel_id=1, source_target_pairs={{0,1},{1,2},{2,3},{3,4},{4,5},{5,6},{6,7},{8,9},{9,10},{10,11},{11... | collective-permute-start | bytes 491528 | tf_op jit(solution)/shard_map/ppermute | solution.py:17
  22.2 4.8 %collective-permute-start.3 = (bf16[5,1,128,128]{3,2,1,0:T(8,128)(2,1)}, bf16[5,1,128,128]{3,2,1,0:T(8,128)(2,1)}, u32[]{:S(2)}, u32[]{:S(2)}) collective-permute-start(bf16[5,1,128,128]{3,2,1,0:T(8,128)(2,1)} %get-tuple-element.373), channel_id=1, source_target_pairs={{1,0},{2,1},{3,2},{4,3},{5,4},{6,5},{7,6},{9,8},{10,9},{11,10},{12... | collective-permute-start | bytes 491528 | tf_op jit(solution)/shard_map/ppermute | solution.py:19
  28.2 172.3 %copy-start.1 = (f32[128]{0:T(128)S(1)}, f32[128]{0:T(128)}, u32[]{:S(2)}) copy-start(f32[128]{0:T(128)} %param.17) | copy-start | bytes 1540
  28.2 173.0 %copy-start.2 = (f32[128]{0:T(128)S(1)}, f32[128]{0:T(128)}, u32[]{:S(2)}) copy-start(f32[128]{0:T(128)} %param.18) | copy-start | bytes 1540
  268.5 77.9 %copy-start.6 = (u32[128]{0:T(128)S(1)}, u32[128]{0:T(128)}, u32[]{:S(2)}) copy-start(u32[128]{0:T(128)} %constant.182) | copy-start | bytes 1540
  271.6 28.7 %copy-start.3 = (f32[2,512,128]{2,1,0:T(8,128)S(1)}, f32[2,512,128]{2,1,0:T(8,128)}, u32[]{:S(2)}) copy-start(f32[2,512,128]{2,1,0:T(8,128)} %get-tuple-element.580) | copy-start | bytes 1572868 | tf_op jit(solution)/shard_map/while
  300.4 0.8 copy-start.4
  308.1 28.7 %copy-start.3 = (f32[2,512,128]{2,1,0:T(8,128)S(1)}, f32[2,512,128]{2,1,0:T(8,128)}, u32[]{:S(2)}) copy-start(f32[2,512,128]{2,1,0:T(8,128)} %get-tuple-element.580) | copy-start | bytes 1572868 | tf_op jit(solution)/shard_map/while
  336.9 0.8 copy-start.4
  341.6 85.0 %copy-start.5 = (s32[1,1,8,128]{3,2,1,0:T(8,128)S(1)}, s32[1,1,8,128]{3,2,1,0:T(8,128)}, u32[]{:S(2)}) copy-start(s32[1,1,8,128]{3,2,1,0:T(8,128)} %param.15) | copy-start | bytes 12292
  342.7 114.2 %reduce-scatter.3.cloned.1.call-start = ((), (), s32[]{:S(2)}) async-start(), calls=%async_computation.1 | async-start | bytes 294912 | tf_op jit(solution)/shard_map/reduce_scatter | solution.py:137
  343.7 4.6 collective-permute-start.4
  345.0 7.3 %collective-permute-start.5 = (bf16[1,3,128,128]{3,2,1,0:T(8,128)(2,1)S(1)}, bf16[1,3,128,128]{3,2,1,0:T(8,128)(2,1)S(1)}, u32[]{:S(2)}, u32[]{:S(2)}) collective-permute-start(bf16[1,3,128,128]{3,2,1,0:T(8,128)(2,1)S(1)} %bitcast.236), channel_id=1, source_target_pairs={{8,0},{16,8},{24,16},{32,24},{40,32},{48,40},{56,48},{64,56},{72,6... | collective-permute-start | bytes 294920 | tf_op jit(solution)/shard_map/ppermute | solution.py:19
  353.3 3.7 collective-permute-start.6
  354.8 4.5 collective-permute-start.7
Sparse Core Ops, SparseCore 0:
  342.8 82.0 all-reduce.4
  427.3 29.5 reduce-scatter.2
where the time goes:
time: 466 us; the launch traced here: 465 us
  blocking collectives  197 us (42%)
  waiting for transfers between devices  104 us (22%)
  matrix products  99.4 us (21%)
  between operations  16.4 us (4%)
  local copies, waits for them, and re-layouts  15.4 us (3%)
  starting transfers between devices  13.9 us (3%)
  other arithmetic  13.7 us (3%)
  loops' own time  5.44 us (1%)
    psum x1, blocking collectives, per_device(): lax.psum((jnp.sum(conv_float * live_mask, axis=0), local_count), ('bx', '...  70.3 us
    unnamed x3, waiting for transfers between devices  64.5 us
    psum x1, blocking collectives, per_device(): lax.psum((jnp.sum(upstream, axis=0), jnp.sum(upstream * normalized, axis=...  64.2 us
    psum x1, blocking collectives, per_device(): lax.psum(jnp.sum(deviation * deviation, axis=0), ('bx', 'by')) / total_count  62.7 us
    dot_general x2, matrix products, backward_block(): jnp.einsum('kbw,bkc->wc', selector, column_grad, precision=lax.Precision....  57.4 us
    reduce_scatter x1, waiting for transfers between devices, per_device(): lax.psum_scatter(partial_x, 'by', scatter_dimension=2, tiled=True)  27 us
    dot_general x2, matrix products, forward_block(): jnp.einsum('kbw,wc->bkc', selector, window, preferred_element_type=jnp.fl...  25.9 us
    ppermute x4, waiting for transfers between devices, extended(): lax.ppermute(head, axis, [((i + 1) % count, i) for i in range(ends)])  12.1 us
  transfers between devices with their start and end apart: 10, of which 6 were waited for; matrix products, arithmetic and copies ran while one was open for 2% of the time, Pallas kernels for 0%

commit v1 on v0

--- a/solution.py
+++ b/solution.py
@@ -95,7 +95,7 @@
     activated = (jnp.maximum(before, 0.0) * live_mask).astype(jnp.bfloat16)
     upstream = cotangent[0, 0].astype(jnp.float32) * (before > 0.0) * live_mask
     sum_up, sum_cross = lax.psum(
-        (jnp.sum(upstream, axis=0), jnp.sum(upstream * normalized, axis=0)), ("bx", "by")
+        lax.psum((jnp.sum(upstream, axis=0), jnp.sum(upstream * normalized, axis=0)), "bx"), "by"
     )
     conv_grad = (
         gain

time: 466 us -> 450 us (0.966)
  blocking collectives: 197 us -> 184 us
    psum x1, blocking collectives: 64.2 us -> 38.1 us  [per_device(): lax.psum((jnp.sum(upstream, axis=0), jnp.sum(upstream * normalized, axis=...]
    psum x0 -> x1, blocking collectives: none -> 12.6 us  [per_device(): lax.psum(lax.psum((jnp.sum(upstream, axis=0), jnp.sum(upstream * normaliz...]
where the time goes in v1:
time: 450 us; the launch traced here: 449 us
  blocking collectives  184 us (41%)
  waiting for transfers between devices  101 us (22%)
  matrix products  99.4 us (22%)
  between operations  16.4 us (4%)
  local copies, waits for them, and re-layouts  15.5 us (3%)
  starting transfers between devices  13.7 us (3%)
  other arithmetic  13.7 us (3%)
  loops' own time  5.44 us (1%)
    psum x1, blocking collectives, per_device(): lax.psum((jnp.sum(conv_float * live_mask, axis=0), local_count), ('bx', '...  70.3 us
    unnamed x3, waiting for transfers between devices  62.7 us
    psum x1, blocking collectives, per_device(): lax.psum(jnp.sum(deviation * deviation, axis=0), ('bx', 'by')) / total_count  62.7 us
    dot_general x2, matrix products, backward_block(): jnp.einsum('kbw,bkc->wc', selector, column_grad, precision=lax.Precision....  57.4 us
    psum x1, blocking collectives, per_device(): lax.psum((jnp.sum(upstream, axis=0), jnp.sum(upstream * normalized, axis=...  38.1 us
    reduce_scatter x1, waiting for transfers between devices, per_device(): lax.psum_scatter(partial_x, 'by', scatter_dimension=2, tiled=True)  27 us
    dot_general x2, matrix products, forward_block(): jnp.einsum('kbw,wc->bkc', selector, window, preferred_element_type=jnp.fl...  25.9 us
    psum x1, blocking collectives, per_device(): lax.psum(lax.psum((jnp.sum(upstream, axis=0), jnp.sum(upstream * normaliz...  12.6 us
  transfers between devices with their start and end apart: 10, of which 6 were waited for; matrix products, arithmetic and copies ran while one was open for 2% of the time, Pallas kernels for 0%

profile of v1, /device:TPU:0, one launch (start us, length us, event | category | flops | bytes accessed | tf_op | source)
XLA Modules:
  0.0 448.9 jit_solution(15977965210708864169)
XLA Ops:
  7.2 1.9 fusion.34
  9.1 3.9 collective-permute-start
  13.0 1.3 collective-permute-start.1
  15.2 4.3 collective-permute-done.1
  20.3 1.9 collective-permute-start.2
  22.2 1.3 collective-permute-start.3
  23.6 1.2 reduce.4
  25.5 1.5 collective-permute-done.3
  27.0 1.1 pad_maximum_fusion
  28.2 38.2 %while.33 = (s32[]{:T(128)}, bf16[2,512,128]{2,1,0:T(8,128)(2,1)S(1)}, bf16[2,512,3456]{1,2,0:T(8,128)(2,1)}, bf16[2,512,128]{2,1,0:T(8,128)(2,1)}, bf16[2,9,64,...) while((s32[]{:T(128)}, ...), condition=%wide.region_1.2_spmd.clone, body=%wide.region_0.1_spmd.sunk.clone | while | flops 4321123840 | bytes 16304801 | solution.py:77
  30.2 0.9 dynamic-slice_bitcast_fusion.3
  31.2 13.0 %fusion.82 = bf16[128,27,512]{2,0,1:T(8,128)(2,1)S(1)} fusion(s32[27,512]{1,0:T(8,128)S(1)} %bitcast_select_fusion.6, bf16[576,128]{1,0:T(8,128)(2,1)S(1)} %bitcast.223, bf16[512,128]{1,0:T(8,128)(2,1)S(1)} %dynamic-slice_bitcast_fusion.3), kind=kOutput, calls=%fused_computation.3.clone.1.clone | convolution fusion | flops 3867738112 | bytes 3872768 | tf_op jit(solution)/shard_map/while/body/eval_jaxpr/kbw,wc->bkc/dot_general | solution.py:71
  44.1 2.0 constant_dynamic-update-slice_fusion.6
  46.1 1.2 fusion.83
  49.3 0.9 dynamic-slice_bitcast_fusion.3
  50.2 13.0 %fusion.82 = bf16[128,27,512]{2,0,1:T(8,128)(2,1)S(1)} fusion(s32[27,512]{1,0:T(8,128)S(1)} %bitcast_select_fusion.6, bf16[576,128]{1,0:T(8,128)(2,1)S(1)} %bitcast.223, bf16[512,128]{1,0:T(8,128)(2,1)S(1)} %dynamic-slice_bitcast_fusion.3), kind=kOutput, calls=%fused_computation.3.clone.1.clone | convolution fusion | flops 3867738112 | bytes 3872768 | tf_op jit(solution)/shard_map/while/body/eval_jaxpr/kbw,wc->bkc/dot_general | solution.py:71
  63.2 2.0 constant_dynamic-update-slice_fusion.6
  65.3 1.2 fusion.83
  66.7 70.3 %all-reduce.1 = (f32[128]{0:T(128)S(1)}, f32[]{:T(128)}) all-reduce(f32[128]{0:T(128)S(1)} %multiply_reduce_fusion.1, f32[]{:T(128)} %fusion.44), channel_id=1, replica_groups=mesh['bx'=16,'by'=8] {'bx','by'}, use_global_device_ids=true, to_apply=%region_3.4 | all-reduce | flops 129 | bytes 1032 | tf_op jit(solution)/shard_map/psum | solution.py:86
  137.8 62.7 %psum.51 = f32[128]{0:T(128)S(1)} all-reduce(f32[128]{0:T(128)S(1)} %multiply_reduce_fusion), channel_id=1, replica_groups=mesh['bx'=16,'by'=8] {'bx','by'}, use_global_device_ids=true, to_apply=%region_7.8 | all-reduce | flops 128 | bytes 1024 | tf_op jit(solution)/shard_map/psum | solution.py:91
  201.2 1.2 fusion.39
  202.4 38.1 %all-reduce.2 = (f32[128]{0:T(128)S(1)}, f32[128]{0:T(128)S(1)}) all-reduce(f32[128]{0:T(128)S(1)} %get-tuple-element.329, f32[128]{0:T(128)S(1)} %get-tuple-element.328), channel_id=1, replica_groups=mesh['bx'=16,'by'=8] {'bx'}, use_global_device_ids=true, to_apply=%region_12.13 | all-reduce | flops 256 | bytes 2048 | tf_op jit(solution)/shard_map/psum | solution.py:98
  240.5 12.6 %all-reduce.3 = (f32[128]{0:T(128)S(1)}, f32[128]{0:T(128)S(1)}) all-reduce(f32[128]{0:T(128)S(1)} %get-tuple-element.366, f32[128]{0:T(128)S(1)} %get-tuple-element.367), channel_id=1, replica_groups=mesh['bx'=16,'by'=8] {'by'}, use_global_device_ids=true, to_apply=%region_13.14 | all-reduce | flops 256 | bytes 2048 | tf_op jit(solution)/shard_map/psum | solution.py:97
  253.1 1.9 fusion.42
  255.0 73.2 %while.34 = (s32[]{:T(128)}, f32[3456,128]{1,0:T(8,128)S(1)}, f32[2,512,128]{2,1,0:T(8,128)}, bf16[2,9,64,128]{3,2,0,1:T(8,128)(2,1)}, bf16[2,512,3456]{1,2,0:T(...) while((s32[]{:T(128)}, f32[3456,128]{1,0:T(8,128)S(1)}, ...), condition=%wide.region_15.16_spmd.clone.clone, body=%wide.region_14.15_spmd.clone.sunk.clone | while | flops 24024522752 | bytes 28413672 | solution.py:130
  256.9 1.1 fusion.89
  258.0 28.7 %fusion.90 = f32[1088,128]{1,0:T(8,128)S(1)} fusion(f32[512,27,128]{2,0,1:T(8,128)S(1)} %fusion.89, s32[27,512]{1,0:T(8,128)S(1)} %bitcast_select_fusion.7), kind=kOutput, calls=%fused_computation.31.clone.1.clone | convolution fusion | flops 23117266944 | bytes 7690240 | tf_op jit(solution)/shard_map/while/body/eval_jaxpr/kbw,bkc->wc/dot_general | solution.py:117
  288.3 3.2 convolution_add_fusion.3
  293.5 1.1 fusion.89
  294.6 28.7 %fusion.90 = f32[1088,128]{1,0:T(8,128)S(1)} fusion(f32[512,27,128]{2,0,1:T(8,128)S(1)} %fusion.89, s32[27,512]{1,0:T(8,128)S(1)} %bitcast_select_fusion.7), kind=kOutput, calls=%fused_computation.31.clone.1.clone | convolution fusion | flops 23117266944 | bytes 7690240 | tf_op jit(solution)/shard_map/while/body/eval_jaxpr/kbw,bkc->wc/dot_general | solution.py:117
  324.9 3.2 convolution_add_fusion.3
  328.1 1.0 convert_element_type.131
  329.2 1.0 fusion.48
  330.2 1.3 collective-permute-start.4
  331.5 1.3 collective-permute-start.5
  334.8 4.4 collective-permute-done.5
  339.2 1.0 pad_maximum_fusion.6
  340.2 1.3 collective-permute-start.6
  341.5 1.3 collective-permute-start.7
  342.8 0.9 multiply_convert_fusion
  343.7 1.1 collective-permute-done.7
  344.8 1.1 pad_maximum_fusion.1
  346.0 62.7 %all-reduce.6.cloned.1.call-done = bf16[27,128,128]{2,1,0:T(8,128)(2,1)} async-done(((bf16[27,128,128]{2,1,0:T(8,128)(2,1)}), bf16[27,128,128]{2,1,0:T(8,128)(2,1)}) %all-reduce.6.cloned.1.call-update) | async-done | bytes 884752
  408.7 0.8 constant_dynamic-slice_fusion.1
  409.5 0.9 copy.30
  410.4 3.2 fusion.35
  413.6 27.0 %reduce-scatter.3.cloned.1.call-done = bf16[27,8,16]{0,1,2:T(8,128)(2,1)} async-done(((bf16[27,8,128]{0,1,2:T(8,128)(2,1)}), bf16[27,8,16]{0,1,2:T(8,128)(2,1)}) %reduce-scatter.3.cloned.1.call-update) | async-done | bytes 6928 | tf_op jit(solution)/shard_map/reduce_scatter | solution.py:137
  440.6 0.8 convert_divide_fusion
  (69 shorter events, 10.6 us)
Async XLA Ops:
  7.2 21.0 %copy-start = (bf16[3456,128]{1,0:T(8,128)(2,1)S(1)}, bf16[3456,128]{1,0:T(8,128)(2,1)}, u32[]{:S(2)}) copy-start(bf16[3456,128]{1,0:T(8,128)(2,1)} %param.16) | copy-start | bytes 2654212
  7.2 401.5 %all-reduce.6.cloned.1.call-start = ((), (), s32[]{:S(2)}) async-start(), calls=%async_computation.2 | async-start | bytes 1769472
  9.1 6.1 %collective-permute-start = (bf16[1,3,128,128]{3,2,1,0:T(8,128)(2,1)S(1)}, bf16[1,3,128,128]{3,2,1,0:T(8,128)(2,1)S(1)}, u32[]{:S(2)}, u32[]{:S(2)}) collective-permute-start(bf16[1,3,128,128]{3,2,1,0:T(8,128)(2,1)S(1)} %bitcast.239), channel_id=1, source_target_pairs={{0,8},{8,16},{16,24},{24,32},{32,40},{40,48},{48,56},{56,64},{64,7... | collective-permute-start | bytes 294920 | tf_op jit(solution)/shard_map/ppermute | solution.py:17
  13.0 6.5 %collective-permute-start.1 = (bf16[1,3,128,128]{3,2,1,0:T(8,128)(2,1)S(1)}, bf16[1,3,128,128]{3,2,1,0:T(8,128)(2,1)S(1)}, u32[]{:S(2)}, u32[]{:S(2)}) collective-permute-start(bf16[1,3,128,128]{3,2,1,0:T(8,128)(2,1)S(1)} %bitcast.238), channel_id=1, source_target_pairs={{8,0},{16,8},{24,16},{32,24},{40,32},{48,40},{56,48},{64,56},{72,6... | collective-permute-start | bytes 294920 | tf_op jit(solution)/shard_map/ppermute | solution.py:19
  20.3 5.2 %collective-permute-start.2 = (bf16[5,1,128,128]{3,2,1,0:T(8,128)(2,1)}, bf16[5,1,128,128]{3,2,1,0:T(8,128)(2,1)}, u32[]{:S(2)}, u32[]{:S(2)}) collective-permute-start(bf16[5,1,128,128]{3,2,1,0:T(8,128)(2,1)} %get-tuple-element.374), channel_id=1, source_target_pairs={{0,1},{1,2},{2,3},{3,4},{4,5},{5,6},{6,7},{8,9},{9,10},{10,11},{11... | collective-permute-start | bytes 491528 | tf_op jit(solution)/shard_map/ppermute | solution.py:17
  22.2 4.8 %collective-permute-start.3 = (bf16[5,1,128,128]{3,2,1,0:T(8,128)(2,1)}, bf16[5,1,128,128]{3,2,1,0:T(8,128)(2,1)}, u32[]{:S(2)}, u32[]{:S(2)}) collective-permute-start(bf16[5,1,128,128]{3,2,1,0:T(8,128)(2,1)} %get-tuple-element.375), channel_id=1, source_target_pairs={{1,0},{2,1},{3,2},{4,3},{5,4},{6,5},{7,6},{9,8},{10,9},{11,10},{12... | collective-permute-start | bytes 491528 | tf_op jit(solution)/shard_map/ppermute | solution.py:19
  28.2 172.3 %copy-start.1 = (f32[128]{0:T(128)S(1)}, f32[128]{0:T(128)}, u32[]{:S(2)}) copy-start(f32[128]{0:T(128)} %param.17) | copy-start | bytes 1540
  28.2 173.0 %copy-start.2 = (f32[128]{0:T(128)S(1)}, f32[128]{0:T(128)}, u32[]{:S(2)}) copy-start(f32[128]{0:T(128)} %param.18) | copy-start | bytes 1540
  254.9 77.9 %copy-start.6 = (u32[128]{0:T(128)S(1)}, u32[128]{0:T(128)}, u32[]{:S(2)}) copy-start(u32[128]{0:T(128)} %constant.182) | copy-start | bytes 1540
  258.0 28.7 %copy-start.3 = (f32[2,512,128]{2,1,0:T(8,128)S(1)}, f32[2,512,128]{2,1,0:T(8,128)}, u32[]{:S(2)}) copy-start(f32[2,512,128]{2,1,0:T(8,128)} %get-tuple-element.582) | copy-start | bytes 1572868 | tf_op jit(solution)/shard_map/while
  286.8 0.8 copy-start.4
  294.6 28.7 %copy-start.3 = (f32[2,512,128]{2,1,0:T(8,128)S(1)}, f32[2,512,128]{2,1,0:T(8,128)}, u32[]{:S(2)}) copy-start(f32[2,512,128]{2,1,0:T(8,128)} %get-tuple-element.582) | copy-start | bytes 1572868 | tf_op jit(solution)/shard_map/while
  323.4 0.8 copy-start.4
  328.1 82.3 %copy-start.5 = (s32[1,1,8,128]{3,2,1,0:T(8,128)S(1)}, s32[1,1,8,128]{3,2,1,0:T(8,128)}, u32[]{:S(2)}) copy-start(s32[1,1,8,128]{3,2,1,0:T(8,128)} %param.15) | copy-start | bytes 12292
  329.2 111.4 %reduce-scatter.3.cloned.1.call-start = ((), (), s32[]{:S(2)}) async-start(), calls=%async_computation.1 | async-start | bytes 294912 | tf_op jit(solution)/shard_map/reduce_scatter | solution.py:137
  330.2 4.6 %collective-permute-start.4 = (bf16[1,3,128,128]{3,2,1,0:T(8,128)(2,1)S(1)}, bf16[1,3,128,128]{3,2,1,0:T(8,128)(2,1)S(1)}, u32[]{:S(2)}, u32[]{:S(2)}) collective-permute-start(bf16[1,3,128,128]{3,2,1,0:T(8,128)(2,1)S(1)} %bitcast.237), channel_id=1, source_target_pairs={{0,8},{8,16},{16,24},{24,32},{32,40},{40,48},{48,56},{56,64},{64,7... | collective-permute-start | bytes 294920 | tf_op jit(solution)/shard_map/ppermute | solution.py:17
  331.5 7.7 %collective-permute-start.5 = (bf16[1,3,128,128]{3,2,1,0:T(8,128)(2,1)S(1)}, bf16[1,3,128,128]{3,2,1,0:T(8,128)(2,1)S(1)}, u32[]{:S(2)}, u32[]{:S(2)}) collective-permute-start(bf16[1,3,128,128]{3,2,1,0:T(8,128)(2,1)S(1)} %bitcast.236), channel_id=1, source_target_pairs={{8,0},{16,8},{24,16},{32,24},{40,32},{48,40},{56,48},{64,56},{72,6... | collective-permute-start | bytes 294920 | tf_op jit(solution)/shard_map/ppermute | solution.py:19
  340.2 3.5 collective-permute-start.6
  341.5 3.3 collective-permute-start.7
Sparse Core Ops, SparseCore 0:
  329.3 79.2 all-reduce.5
  411.0 29.5 reduce-scatter.2
